TPU v7x, 32 devices: a whole 2x2x4 slice. The times are simulated.
32 devices in a mesh: cols: 32 (over z, y, x, core).
Axes of the slice: x: 2, y: 2, z: 4, core: 2. Of those that a mesh axis runs over, the one named last changes fastest.
Arguments:
- gcm_state: float32 [2, 72, 16384], P(None, None, 'cols'), may hold values from -6 to 6
- crm_state: bfloat16 [2, 58, 32, 16384], P(None, None, None, 'cols'), may hold values from -6 to 6
- span_map: int32 [16384], P('cols'), may hold values from 0 to 16383, as said below
- crm_cost: int32 [16384], P('cols'), may hold values from 1 to 58
- neighbours: int32 [4096, 8], P('cols'), may hold values from -1 to 4095, as said below
Outputs:
- crm_next: bfloat16 [2, 58, 32, 16384], P(None, None, None, 'cols')
- smoothed: float32 [2, 72, 16384], P(None, None, 'cols')
Inputs may be any that keep to these rules, and one draw needn't show every extreme that they name: `span_map`: A permutation of the span positions; position p is held by device p // 512. The columns of each device go, exactly 32 each, to 16 distinct devices, its own among them, and each device receives exactly 32 columns from each of 16 devices. `neighbours`: -1 marks an empty slot and stands only in the last slot; every other entry names an element of the element's own device or of one of the two devices beside it along cols, wrapping around.
All inputs are finite; a program needn't handle non-finite values.
Results may differ from a plain program's by a relative error of at most 0.001.
Values sent between devices are 32-bit elements; how exact they have to be, the bound alone decides.
A program may use at most 128 MiB of HBM per device.

v0:
```python
import jax
import jax.numpy as jnp
from jax import lax
from jax.sharding import PartitionSpec as P

LEV = 72
CRM_LEV = 58
PCOL = 4
NBR = 8
SUBSTEPS = 2
RELAX = 0.5
STEP = 0.5
MIXING = 0.2
LATENT = 0.6
SMOOTHING = 0.5


def padded(shard, sides, width):
    for axis, dim in sides:
        size, length = (lax.axis_size(axis), shard.shape[dim])
        up = [(i, (i + 1) % size) for i in range(size)]
        down = [(j, i) for i, j in up]
        last = lax.slice_in_dim(shard, length - width, length, axis=dim)
        first = lax.slice_in_dim(shard, 0, width, axis=dim)
        before = lax.ppermute(last, axis, up)
        after = lax.ppermute(first, axis, down)
        shard = jnp.concatenate([before, shard, after], axis=dim)
    return shard


def interpolation(rows_out, rows_in):
    target = jnp.arange(rows_out, dtype=jnp.int32)[:, None]
    source = jnp.arange(rows_in, dtype=jnp.int32)[None, :]
    scaled = target * (rows_in - 1)
    lower = scaled // (rows_out - 1)
    weight = (scaled - lower * (rows_out - 1)).astype(jnp.float32) / (rows_out - 1)
    upper = jnp.minimum(lower + 1, rows_in - 1)
    return jnp.where(source == lower, 1.0 - weight, 0.0) + jnp.where(source == upper, weight, 0.0)


def crm_steps(fields, forcing, active):
    levels = fields.shape[1]
    height = jnp.arange(levels, dtype=jnp.float32)
    saturation = (1.0 - 0.8 * height / (levels - 1))[:, None, None]
    for substep in range(SUBSTEPS):
        sideways = jnp.roll(fields, 1, axis=2) + jnp.roll(fields, -1, axis=2) - 2.0 * fields
        upper_cells = jnp.concatenate([fields[:, 1:], fields[:, -1:]], axis=1)
        lower_cells = jnp.concatenate([fields[:, :1], fields[:, :-1]], axis=1)
        vertical = upper_cells + lower_cells - 2.0 * fields
        fields = fields + STEP * (forcing[:, :, None, :] + MIXING * (sideways + vertical))
        condensed = jnp.maximum(fields[1] - saturation, 0.0) * active[:, None, :]
        fields = jnp.stack([fields[0] + LATENT * condensed, fields[1] - condensed])
    return fields


def physics(crm_old, profile, cloud_top):
    start = crm_old.astype(jnp.float32)
    start_mean = jnp.mean(start, axis=2)
    forcing = RELAX * (profile - start_mean)
    levels = crm_old.shape[1]
    active = (jnp.arange(levels, dtype=jnp.int32)[:, None] < cloud_top[None, :]).astype(jnp.float32)
    final = crm_steps(start, forcing, active)
    change = jnp.mean(final, axis=2) - start_mean
    return (final.astype(jnp.bfloat16), change)


def element_mean(values, elements):
    return jnp.mean(values.reshape(2 * LEV, elements, PCOL), axis=2)


def on_device(gcm_state, crm_state, span_map, crm_cost, neighbours):
    devices = lax.axis_size("cols")
    device = lax.axis_index("cols")
    columns = gcm_state.shape[2]
    elements = neighbours.shape[0]
    capacity = 2 * columns // devices
    interp_down = interpolation(CRM_LEV, LEV)
    interp_up = interpolation(LEV, CRM_LEV)
    target = span_map // columns
    span_slot = span_map % columns
    peer_ids = jnp.arange(devices, dtype=jnp.int32)
    onehot = (target[:, None] == peer_ids[None, :]).astype(jnp.int32)
    before = jnp.cumsum(onehot, axis=0) - onehot
    within = jnp.sum(before * onehot, axis=1)
    position = target * capacity + within
    outgoing = gcm_state.reshape(2 * LEV, columns)
    row_count = outgoing.shape[0]
    slot_total = devices * capacity
    send_rows = jnp.zeros((row_count, slot_total), jnp.float32).at[:, position].set(outgoing)
    labels = jnp.stack([span_slot, crm_cost]).astype(jnp.float32)
    empty_labels = jnp.stack(
        [jnp.full((slot_total,), columns, jnp.float32), jnp.zeros((slot_total,), jnp.float32)]
    )
    send_labels = empty_labels.at[:, position].set(labels)
    arrived, arrived_labels = (
        lax.all_to_all(send_rows, "cols", split_axis=1, concat_axis=1, tiled=True),
        lax.all_to_all(send_labels, "cols", split_axis=1, concat_axis=1, tiled=True),
    )
    arrived_slot = arrived_labels[0].astype(jnp.int32)
    placed = (
        jnp.zeros((row_count, columns + 1), jnp.float32)
        .at[:, arrived_slot]
        .set(arrived)[:, :columns]
    )
    span_top = (
        jnp.zeros((columns + 1,), jnp.int32)
        .at[arrived_slot]
        .set(arrived_labels[1].astype(jnp.int32))[:columns]
    )
    span_profile = jnp.einsum(
        "jk,fkc->fjc", interp_down, placed.reshape(2, LEV, columns), precision=lax.Precision.HIGHEST
    )
    crm_next, change = physics(crm_state, span_profile, span_top)
    returning = jnp.einsum(
        "kj,fjc->fkc", interp_up, change, precision=lax.Precision.HIGHEST
    ).reshape(2 * LEV, columns)
    source_slot = jnp.minimum(arrived_slot, columns - 1)
    returned = lax.all_to_all(
        returning[:, source_slot], "cols", split_axis=1, concat_axis=1, tiled=True
    )
    own_rows = returned[:, position]
    tendency = own_rows.reshape(2, LEV, columns)
    updated = gcm_state + tendency
    edge_mean = element_mean(updated, elements)
    extended = padded(edge_mean, (("cols", 1),), elements)
    valid = neighbours >= 0
    offset = jnp.mod(neighbours - (device - 1) * elements, devices * elements)
    lookup = jnp.where(valid, offset, 0)
    gathered = jnp.take(extended, lookup.reshape(-1), axis=1).reshape(2 * LEV, elements, NBR)
    gathered = gathered * valid.astype(jnp.float32)[None]
    neighbour_sum = jnp.sum(gathered, axis=2)
    count = jnp.sum(valid.astype(jnp.float32), axis=1)
    pull = SMOOTHING * (neighbour_sum / count[None, :] - edge_mean)
    smoothed = (updated.reshape(2 * LEV, elements, PCOL) + pull[:, :, None]).reshape(
        2, LEV, columns
    )
    return (crm_next, smoothed)


def solution(mesh):
    placed = (
        P(None, None, "cols"),
        P(None, None, None, "cols"),
        P("cols"),
        P("cols"),
        P("cols", None),
    )
    return jax.shard_map(
        on_device,
        mesh=mesh,
        in_specs=placed,
        out_specs=(P(None, None, None, "cols"), P(None, None, "cols")),
        check_vma=False,
    )
```

profile of v0, /device:TPU:0, one launch (start us, length us, event | category | flops | bytes accessed | tf_op | source)
XLA Modules:
  0.0 169.9 jit_solution(7699775522284530339)
XLA Ops:
  0.6 0.7 add_select_fusion.1
  1.3 1.2 reduce-window.6
  2.9 0.7 fusion.67
  3.7 1.0 copy.42
  4.8 1.9 %scatter_fusion = f32[2,1024]{0,1:T(8,128)S(1)} fusion(f32[2,1024]{0,1:T(8,128)S(1)} %copy.42, s32[512]{0:T(512)S(1)} %compare_select_fusion.4, f32[512,2]{1,0:T(8,128)S(1)} %copy.27), kind=kCustom, calls=%fused_computation.3 | custom fusion | bytes 14336 | tf_op jit(solution)/shard_map/scatter | solution.py:94
  6.7 0.9 copy.28
  7.6 7.3 %all-to-all-start = ((f32[2,32,32]{2,0,1:T(2,128)}), f32[2,32,32]{2,0,1:T(2,128)S(1)}, u32[]{:S(2)}, u32[]{:S(2)}) async-start(f32[2,32,32]{2,0,1:T(2,128)} %copy.28), calls=%async_computation | async-start | bytes 65536 | tf_op jit(solution)/shard_map/all_to_all | solution.py:97
  14.9 11.3 %fusion.79 = (f32[2,58,31,512]{3,2,1,0:T(8,128)}, f32[2,58,31,512]{3,2,1,0:T(8,128)}) fusion(bf16[2,58,32,512]{3,2,1,0:T(8,128)(2,1)} %param.6), kind=kLoop, calls=%fused_computation.161 | loop fusion | bytes 29458432 | tf_op jit(solution)/shard_map/jit(_roll_static)/slice | solution.py:46
  26.2 7.3 %fusion.78 = (f32[2,57,32,512]{3,2,1,0:T(8,128)}, f32[2,57,32,512]{3,2,1,0:T(8,128)}) fusion(bf16[2,58,32,512]{3,2,1,0:T(8,128)(2,1)S(1)} %copy-done), kind=kLoop, calls=%fused_computation.160 | loop fusion | bytes 29884416 | tf_op jit(solution)/shard_map/slice | solution.py:48
  34.1 3.3 %scatter_custom_fusion.1 = f32[144,1024]{0,1:T(8,128)} fusion(s32[512]{0:T(512)S(1)} %compare_select_fusion.4, f32[144,512]{0,1:T(8,128)S(1)} %copy.29, f32[]{:T(128)} %constant.56.clone.1), kind=kCustom, calls=%fused_computation.62 | custom fusion | bytes 1114116 | tf_op jit(solution)/shard_map/scatter | solution.py:89
  37.4 5.8 %all-to-all-start.1 = ((f32[144,32,32]{0,2,1:T(8,128)}), f32[144,32,32]{0,2,1:T(8,128)S(1)}, u32[]{:S(2)}, u32[]{:S(2)}) async-start(f32[144,32,32]{0,2,1:T(8,128)} %bitcast.9), calls=%async_computation.1 | async-start | bytes 2097152 | tf_op jit(solution)/shard_map/all_to_all | solution.py:96
  43.3 3.4 %convert_reduce_fusion = f32[2,58,512]{2,1,0:T(8,128)S(1)} fusion(bf16[2,58,32,512]{3,2,1,0:T(8,128)(2,1)} %param.6), kind=kLoop, calls=%fused_computation.55 | loop fusion | flops 3741696 | bytes 4038656 | tf_op jit(solution)/shard_map/reduce_sum | solution.py:58
  46.9 4.3 %scatter_custom_fusion.3 = s32[513]{0:T(1024)S(1)} fusion(s32[1024]{0:T(1024)S(1)} %bitcast.83, s32[1024]{0:T(1024)S(1)} %reshape.308, s32[]{:T(128)} %constant.62.clone.1), kind=kCustom, calls=%fused_computation.139 | custom fusion | bytes 2056 | tf_op jit(solution)/shard_map/scatter | solution.py:108
  51.3 18.2 %all-to-all-done.1 = f32[144,32,32]{0,2,1:T(8,128)S(1)} async-done(((f32[144,32,32]{0,2,1:T(8,128)}), f32[144,32,32]{0,2,1:T(8,128)S(1)}, u32[]{:S(2)}, u32[]{:S(2)}) %all-to-all-start.1) | async-done | bytes 589856 | tf_op jit(solution)/shard_map/all_to_all | solution.py:96
  69.5 5.1 %scatter_custom_fusion.2 = f32[144,513]{0,1:T(8,128)S(1)} fusion(s32[1024]{0:T(1024)S(1)} %bitcast.84, f32[1024,144]{1,0:T(8,128)S(1)} %bitcast.78, f32[]{:T(128)} %constant.56.clone.1), kind=kCustom, calls=%fused_computation.66 | custom fusion | bytes 295492 | tf_op jit(solution)/shard_map/scatter | solution.py:103
  75.2 13.5 %fusion.7 = f32[2,58,32,512]{3,2,1,0:T(8,128)S(1)} fusion(f32[2,58,31,512]{3,2,1,0:T(8,128)} %get-tuple-element.23, f32[2,58,1,512]{3,2,1,0:T(1,128)S(1)} %get-tuple-element.25, f32[2,58,1,512]{3,2,1,0:T(1,128)S(1)} %get-tuple-element.24, f32[2,58,31,512]{3,2,1,0:T(8,128)} %get-tuple-element.22, f32[2,1,32,512]{3,2,1,0:T(8,128)S(1)} %get-tuple-element.19, ...), kind=kLoop, calls=%fused_computation.32 | loop fusion | flops 28508160 | bytes 42049536 | tf_op jit(solution)/shard_map/add | solution.py:50
  88.8 1.5 fusion.21
  90.3 6.1 %fusion.17 = (f32[2,57,32,512]{3,2,1,0:T(8,128)}, f32[2,57,32,512]{3,2,1,0:T(8,128)}) fusion(f32[1,58,32,512]{3,2,1,0:T(8,128)S(1)} %get-tuple-element.9, f32[1,58,32,512]{3,2,1,0:T(8,128)S(1)} %get-tuple-element.8), kind=kLoop, calls=%fused_computation.46 | loop fusion | flops 3735552 | bytes 22544384 | tf_op jit(solution)/shard_map/stack | solution.py:52
  96.8 4.0 %fusion.1 = (f32[2,58,31,512]{3,2,1,0:T(8,128)S(1)}, f32[2,58,31,512]{3,2,1,0:T(8,128)}) fusion(f32[1,58,32,512]{3,2,1,0:T(8,128)S(1)} %get-tuple-element.9, f32[1,58,32,512]{3,2,1,0:T(8,128)S(1)} %get-tuple-element.8), kind=kLoop, calls=%fused_computation.25 | loop fusion | flops 3682304 | bytes 22331392 | tf_op jit(solution)/shard_map/stack | solution.py:52
  100.9 9.7 %fusion.14 = f32[2,58,32,512]{3,2,1,0:T(8,128)S(1)} fusion(f32[2,58,31,512]{3,2,1,0:T(8,128)} %get-tuple-element.15, f32[2,58,1,512]{3,2,1,0:T(1,128)S(1)} %get-tuple-element.17, f32[2,58,1,512]{3,2,1,0:T(1,128)S(1)} %get-tuple-element.16, f32[2,58,31,512]{3,2,1,0:T(8,128)S(1)} %get-tuple-element.14, f32[1,58,32,512]{3,2,1,0:T(8,128)S(1)} %get-tuple-element.8, ...), kind=kLoop, calls=%fused_computation.41 | loop fusion | flops 28508160 | bytes 45850624 | tf_op jit(solution)/shard_map/add | solution.py:50
  110.5 1.9 %slice_add_fusion = (f32[1,58,32,512]{3,2,1,0:T(8,128)S(1)}, f32[1,58,32,512]{3,2,1,0:T(8,128)S(1)}) fusion(f32[2,58,32,512]{3,2,1,0:T(8,128)S(1)} %fusion.14, f32[58,512]{1,0:T(8,128)S(1)} %fusion.40, f32[58]{0:T(128)S(1)} %multiply_subtract_fusion), kind=kLoop, calls=%fused_computation.49 | loop fusion | flops 5701632 | bytes 15323368 | tf_op jit(solution)/shard_map/add | solution.py:52
  112.5 1.5 fusion.18
  114.5 0.9 copy-done.2
  115.6 4.7 %gather_fusion = f32[1024,144]{1,0:T(8,128)} fusion(f32[144,512]{0,1:T(8,128)S(1)} %copy.31, s32[1024]{0:T(1024)S(1)} %broadcast_clamp_fusion.1), kind=kCustom, calls=%fused_computation | custom fusion | bytes 1183744 | tf_op jit(solution)/shard_map/gather | solution.py:119
  120.3 3.8 %all-to-all-start.2 = ((f32[144,32,32]{0,2,1:T(8,128)}), f32[144,32,32]{0,2,1:T(8,128)S(1)}, u32[]{:S(2)}, u32[]{:S(2)}) async-start(f32[144,32,32]{0,2,1:T(8,128)} %bitcast.20), calls=%async_computation.2 | async-start | bytes 2097152 | tf_op jit(solution)/shard_map/all_to_all | solution.py:118
  124.6 25.5 %all-to-all-done.2 = f32[144,32,32]{0,2,1:T(8,128)S(1)} async-done(((f32[144,32,32]{0,2,1:T(8,128)}), f32[144,32,32]{0,2,1:T(8,128)S(1)}, u32[]{:S(2)}, u32[]{:S(2)}) %all-to-all-start.2) | async-done | bytes 589856 | tf_op jit(solution)/shard_map/all_to_all | solution.py:118
  150.1 1.6 gather_fusion.1
  153.0 5.3 %collective-permute-start.1 = (f32[144,128]{0,1:T(8,128)S(1)}, f32[144,128]{0,1:T(8,128)S(1)}, u32[]{:S(2)}, u32[]{:S(2)}) collective-permute-start(f32[144,128]{0,1:T(8,128)S(1)} %broadcast_multiply_fusion), channel_id=1, source_target_pairs={{1,0},{2,1},{3,2},{4,3},{5,4},{6,5},{7,6},{8,7},{9,8},{10,9},{11,1... | collective-permute-start | bytes 221192 | tf_op jit(solution)/shard_map/ppermute | solution.py:26
  158.4 5.8 %fusion.19 = bf16[2,58,32,512]{3,2,1,0:T(8,128)(2,1)} fusion(f32[1,58,32,512]{3,2,1,0:T(8,128)} %copy-done.2, f32[1,58,32,512]{3,2,1,0:T(8,128)} %copy-done.1), kind=kLoop, calls=%fused_computation.48 | loop fusion | flops 1900544 | bytes 11403264 | tf_op jit(solution)/shard_map/convert_element_type | solution.py:64
  164.2 3.5 %gather_fusion.2 = f32[1024,144]{1,0:T(8,128)S(1)} fusion(f32[144,384]{0,1:T(8,128)S(1)} %pad_maximum_fusion.2, s32[1024]{0:T(1024)S(1)} %broadcast_clamp_fusion), kind=kCustom, calls=%fused_computation.2 | custom fusion | bytes 1183744 | tf_op jit(solution)/shard_map/jit(_take)/gather | solution.py:129
  167.6 0.7 fusion.25
  169.2 0.8 add.213
  (62 shorter events, 5.9 us)
Async XLA Ops:
  7.6 29.8 %all-to-all-start = ((f32[2,32,32]{2,0,1:T(2,128)}), f32[2,32,32]{2,0,1:T(2,128)S(1)}, u32[]{:S(2)}, u32[]{:S(2)}) async-start(f32[2,32,32]{2,0,1:T(2,128)} %copy.28), calls=%async_computation | async-start | bytes 65536 | tf_op jit(solution)/shard_map/all_to_all | solution.py:97
  14.9 11.3 %copy-start = (bf16[2,58,32,512]{3,2,1,0:T(8,128)(2,1)S(1)}, bf16[2,58,32,512]{3,2,1,0:T(8,128)(2,1)}, u32[]{:S(2)}) copy-start(bf16[2,58,32,512]{3,2,1,0:T(8,128)(2,1)} %param.6) | copy-start | bytes 11403268
  26.2 7.7 %copy-start.3 = (f32[2,72,512]{2,1,0:T(8,128)S(1)}, f32[2,72,512]{2,1,0:T(8,128)}, u32[]{:S(2)}) copy-start(f32[2,72,512]{2,1,0:T(8,128)} %param.5) | copy-start | bytes 884740
  37.4 32.1 %all-to-all-start.1 = ((f32[144,32,32]{0,2,1:T(8,128)}), f32[144,32,32]{0,2,1:T(8,128)S(1)}, u32[]{:S(2)}, u32[]{:S(2)}) async-start(f32[144,32,32]{0,2,1:T(8,128)} %bitcast.9), calls=%async_computation.1 | async-start | bytes 2097152 | tf_op jit(solution)/shard_map/all_to_all | solution.py:96
  112.4 2.0 %copy-start.1 = (f32[1,58,32,512]{3,2,1,0:T(8,128)}, f32[1,58,32,512]{3,2,1,0:T(8,128)S(1)}, u32[]{:S(2)}) copy-start(f32[1,58,32,512]{3,2,1,0:T(8,128)S(1)} %get-tuple-element.6) | copy-start | bytes 11403268
  112.5 2.9 %copy-start.2 = (f32[1,58,32,512]{3,2,1,0:T(8,128)}, f32[1,58,32,512]{3,2,1,0:T(8,128)S(1)}, u32[]{:S(2)}) copy-start(f32[1,58,32,512]{3,2,1,0:T(8,128)S(1)} %get-tuple-element.7) | copy-start | bytes 11403268
  112.5 11.7 %copy-start.4 = (s32[128,8]{0,1:T(8,128)S(1)}, s32[128,8]{0,1:T(8,128)}, u32[]{:S(2)}) copy-start(s32[128,8]{0,1:T(8,128)} %param.9) | copy-start | bytes 12292
  120.3 29.9 %all-to-all-start.2 = ((f32[144,32,32]{0,2,1:T(8,128)}), f32[144,32,32]{0,2,1:T(8,128)S(1)}, u32[]{:S(2)}, u32[]{:S(2)}) async-start(f32[144,32,32]{0,2,1:T(8,128)} %bitcast.20), calls=%async_computation.2 | async-start | bytes 2097152 | tf_op jit(solution)/shard_map/all_to_all | solution.py:118
  153.0 11.2 %collective-permute-start = (f32[144,128]{0,1:T(8,128)S(1)}, f32[144,128]{0,1:T(8,128)S(1)}, u32[]{:S(2)}, u32[]{:S(2)}) collective-permute-start(f32[144,128]{0,1:T(8,128)S(1)} %broadcast_multiply_fusion), channel_id=1, source_target_pairs={{0,1},{1,2},{2,3},{3,4},{4,5},{5,6},{6,7},{7,8},{8,9},{9,10},{10,1... | collective-permute-start | bytes 221192 | tf_op jit(solution)/shard_map/ppermute | solution.py:25
  153.0 11.1 %collective-permute-start.1 = (f32[144,128]{0,1:T(8,128)S(1)}, f32[144,128]{0,1:T(8,128)S(1)}, u32[]{:S(2)}, u32[]{:S(2)}) collective-permute-start(f32[144,128]{0,1:T(8,128)S(1)} %broadcast_multiply_fusion), channel_id=1, source_target_pairs={{1,0},{2,1},{3,2},{4,3},{5,4},{6,5},{7,6},{8,7},{9,8},{10,9},{11,1... | collective-permute-start | bytes 221192 | tf_op jit(solution)/shard_map/ppermute | solution.py:26
where the time goes:
time: 170 us
  other arithmetic  52.7 us (31%)
  local copies, waits for them, and re-layouts  49.2 us (29%)
  waiting for transfers between devices  43.7 us (26%)
  starting transfers between devices  22.3 us (13%)
    all_to_all x1, waiting for transfers between devices, on_device(): lax.all_to_all(returning[:, source_slot], 'cols', split_axis=1, concat_ax...  25.5 us
    add x2, other arithmetic, crm_steps(): fields + STEP * (forcing[:, :, None, :] + MIXING * (sideways + vertical))  23.2 us
    all_to_all x1, waiting for transfers between devices, on_device(): lax.all_to_all(send_rows, 'cols', split_axis=1, concat_axis=1, tiled=True)  18.2 us
    slice x2, local copies, waits for them, and re-layouts, crm_steps(): jnp.roll(fields, -1, axis=2)  11.6 us
    another operation x4, other arithmetic, crm_steps(): fields = jnp.stack([fields[0] + LATENT * condensed, fields[1] - condensed])  10.6 us
    slice x2, local copies, waits for them, and re-layouts, crm_steps(): lower_cells = jnp.concatenate([fields[:, :1], fields[:, :-1]], axis=1)  7.31 us
    all_to_all x1, starting transfers between devices, on_device(): lax.all_to_all(send_labels, 'cols', split_axis=1, concat_axis=1, tiled=True)  7.3 us
    all_to_all x1, starting transfers between devices, on_device(): lax.all_to_all(send_rows, 'cols', split_axis=1, concat_axis=1, tiled=True)  5.83 us
  transfers between devices with their start and end apart: 5, of which 2 were waited for; matrix products, arithmetic and copies ran while one was open for 22% of the time, Pallas kernels for 0%

commit v1 on v0

--- a/solution.py
+++ b/solution.py
@@ -115,9 +115,10 @@
         "kj,fjc->fkc", interp_up, change, precision=lax.Precision.HIGHEST
     ).reshape(2 * LEV, columns)
     source_slot = jnp.minimum(arrived_slot, columns - 1)
-    returned = lax.all_to_all(
-        returning[:, source_slot], "cols", split_axis=1, concat_axis=1, tiled=True
-    )
+    x = returning[:, source_slot]
+    pieces = jnp.split(x, lax.axis_size("cols"), axis=1)
+    received = lax.all_to_all(jnp.stack(pieces), "cols", 0, 0)
+    returned = jnp.concatenate(received, axis=1)
     own_rows = returned[:, position]
     tendency = own_rows.reshape(2, LEV, columns)
     updated = gcm_state + tendency

time: 170 us -> 189 us (1.11)
  local copies, waits for them, and re-layouts: 49.2 us -> 67.7 us
    unnamed x11 -> x42, local copies, waits for them, and re-layouts: 2.02 us -> 21.1 us
  transfers between devices with their start and end apart: 5 -> 5, of which waited for: 2 -> 2; matrix products, arithmetic and copies ran while one was open for 22% -> 19% of each run, Pallas kernels for 0% -> 0%
where the time goes in v1:
time: 189 us; the launch traced here: 188 us
  local copies, waits for them, and re-layouts  67.7 us (36%)
  other arithmetic  52.7 us (28%)
  waiting for transfers between devices  43.9 us (23%)
  starting transfers between devices  22.1 us (12%)
    all_to_all x1, waiting for transfers between devices, on_device(): received = lax.all_to_all(jnp.stack(pieces), 'cols', 0, 0)  25.7 us
    add x2, other arithmetic, crm_steps(): fields + STEP * (forcing[:, :, None, :] + MIXING * (sideways + vertical))  23.2 us
    unnamed x42, local copies, waits for them, and re-layouts  21.1 us
    all_to_all x1, waiting for transfers between devices, on_device(): lax.all_to_all(send_rows, 'cols', split_axis=1, concat_axis=1, tiled=True)  18.2 us
    slice x2, local copies, waits for them, and re-layouts, crm_steps(): jnp.roll(fields, -1, axis=2)  11.6 us
    another operation x4, other arithmetic, crm_steps(): fields = jnp.stack([fields[0] + LATENT * condensed, fields[1] - condensed])  10.6 us
    slice x2, local copies, waits for them, and re-layouts, crm_steps(): lower_cells = jnp.concatenate([fields[:, :1], fields[:, :-1]], axis=1)  7.31 us
    all_to_all x1, starting transfers between devices, on_device(): lax.all_to_all(send_labels, 'cols', split_axis=1, concat_axis=1, tiled=True)  7.3 us
  transfers between devices with their start and end apart: 5, of which 2 were waited for; matrix products, arithmetic and copies ran while one was open for 19% of the time, Pallas kernels for 0%

profile of v1, /device:TPU:0, one launch (start us, length us, event | category | flops | bytes accessed | tf_op | source)
XLA Modules:
  0.0 188.5 jit_solution(8146383987474895465)
XLA Ops:
  0.6 0.7 add_select_fusion.1
  1.3 1.2 reduce-window.6
  2.9 0.7 fusion.67
  3.7 1.0 copy.73
  4.8 1.9 %scatter_fusion = f32[2,1024]{0,1:T(8,128)S(1)} fusion(f32[2,1024]{0,1:T(8,128)S(1)} %copy.73, s32[512]{0:T(512)S(1)} %compare_select_fusion.4, f32[512,2]{1,0:T(8,128)S(1)} %copy.27), kind=kCustom, calls=%fused_computation.3 | custom fusion | bytes 14336 | tf_op jit(solution)/shard_map/scatter | solution.py:94
  6.7 0.9 copy.28
  7.6 7.3 %all-to-all-start = ((f32[2,32,32]{2,0,1:T(2,128)}), f32[2,32,32]{2,0,1:T(2,128)S(1)}, u32[]{:S(2)}, u32[]{:S(2)}) async-start(f32[2,32,32]{2,0,1:T(2,128)} %copy.28), calls=%async_computation | async-start | bytes 65536 | tf_op jit(solution)/shard_map/all_to_all | solution.py:97
  14.9 11.3 %fusion.79 = (f32[2,58,31,512]{3,2,1,0:T(8,128)}, f32[2,58,31,512]{3,2,1,0:T(8,128)}) fusion(bf16[2,58,32,512]{3,2,1,0:T(8,128)(2,1)} %param.6), kind=kLoop, calls=%fused_computation.225 | loop fusion | bytes 29458432 | tf_op jit(solution)/shard_map/jit(_roll_static)/slice | solution.py:46
  26.2 7.3 %fusion.78 = (f32[2,57,32,512]{3,2,1,0:T(8,128)}, f32[2,57,32,512]{3,2,1,0:T(8,128)}) fusion(bf16[2,58,32,512]{3,2,1,0:T(8,128)(2,1)S(1)} %copy-done), kind=kLoop, calls=%fused_computation.224 | loop fusion | bytes 29884416 | tf_op jit(solution)/shard_map/slice | solution.py:48
  34.1 3.3 %scatter_custom_fusion.1 = f32[144,1024]{0,1:T(8,128)} fusion(s32[512]{0:T(512)S(1)} %compare_select_fusion.4, f32[144,512]{0,1:T(8,128)S(1)} %copy.29, f32[]{:T(128)} %constant.56.clone.1), kind=kCustom, calls=%fused_computation.62 | custom fusion | bytes 1114116 | tf_op jit(solution)/shard_map/scatter | solution.py:89
  37.4 5.8 %all-to-all-start.1 = ((f32[144,32,32]{0,2,1:T(8,128)}), f32[144,32,32]{0,2,1:T(8,128)S(1)}, u32[]{:S(2)}, u32[]{:S(2)}) async-start(f32[144,32,32]{0,2,1:T(8,128)} %bitcast.9), calls=%async_computation.1 | async-start | bytes 2097152 | tf_op jit(solution)/shard_map/all_to_all | solution.py:96
  43.3 3.4 %convert_reduce_fusion = f32[2,58,512]{2,1,0:T(8,128)S(1)} fusion(bf16[2,58,32,512]{3,2,1,0:T(8,128)(2,1)} %param.6), kind=kLoop, calls=%fused_computation.55 | loop fusion | flops 3741696 | bytes 4038656 | tf_op jit(solution)/shard_map/reduce_sum | solution.py:58
  46.9 4.3 %scatter_custom_fusion.3 = s32[513]{0:T(1024)S(1)} fusion(s32[1024]{0:T(1024)S(1)} %bitcast.243, s32[1024]{0:T(1024)S(1)} %reshape.314, s32[]{:T(128)} %constant.62.clone.1), kind=kCustom, calls=%fused_computation.203 | custom fusion | bytes 2056 | tf_op jit(solution)/shard_map/scatter | solution.py:108
  51.3 18.2 %all-to-all-done.1 = f32[144,32,32]{0,2,1:T(8,128)S(1)} async-done(((f32[144,32,32]{0,2,1:T(8,128)}), f32[144,32,32]{0,2,1:T(8,128)S(1)}, u32[]{:S(2)}, u32[]{:S(2)}) %all-to-all-start.1) | async-done | bytes 589856 | tf_op jit(solution)/shard_map/all_to_all | solution.py:96
  69.5 5.1 %scatter_custom_fusion.2 = f32[144,513]{0,1:T(8,128)S(1)} fusion(s32[1024]{0:T(1024)S(1)} %bitcast.244, f32[1024,144]{1,0:T(8,128)S(1)} %bitcast.238, f32[]{:T(128)} %constant.56.clone.1), kind=kCustom, calls=%fused_computation.66 | custom fusion | bytes 295492 | tf_op jit(solution)/shard_map/scatter | solution.py:103
  75.2 13.5 %fusion.7 = f32[2,58,32,512]{3,2,1,0:T(8,128)S(1)} fusion(f32[2,58,31,512]{3,2,1,0:T(8,128)} %get-tuple-element.23, f32[2,58,1,512]{3,2,1,0:T(1,128)S(1)} %get-tuple-element.25, f32[2,58,1,512]{3,2,1,0:T(1,128)S(1)} %get-tuple-element.24, f32[2,58,31,512]{3,2,1,0:T(8,128)} %get-tuple-element.22, f32[2,1,32,512]{3,2,1,0:T(8,128)S(1)} %get-tuple-element.19, ...), kind=kLoop, calls=%fused_computation.32 | loop fusion | flops 28508160 | bytes 42049536 | tf_op jit(solution)/shard_map/add | solution.py:50
  88.8 1.5 fusion.21
  90.3 6.1 %fusion.17 = (f32[2,57,32,512]{3,2,1,0:T(8,128)}, f32[2,57,32,512]{3,2,1,0:T(8,128)}) fusion(f32[1,58,32,512]{3,2,1,0:T(8,128)S(1)} %get-tuple-element.9, f32[1,58,32,512]{3,2,1,0:T(8,128)S(1)} %get-tuple-element.8), kind=kLoop, calls=%fused_computation.46 | loop fusion | flops 3735552 | bytes 22544384 | tf_op jit(solution)/shard_map/stack | solution.py:52
  96.8 4.0 %fusion.1 = (f32[2,58,31,512]{3,2,1,0:T(8,128)S(1)}, f32[2,58,31,512]{3,2,1,0:T(8,128)}) fusion(f32[1,58,32,512]{3,2,1,0:T(8,128)S(1)} %get-tuple-element.9, f32[1,58,32,512]{3,2,1,0:T(8,128)S(1)} %get-tuple-element.8), kind=kLoop, calls=%fused_computation.25 | loop fusion | flops 3682304 | bytes 22331392 | tf_op jit(solution)/shard_map/stack | solution.py:52
  100.9 9.7 %fusion.14 = f32[2,58,32,512]{3,2,1,0:T(8,128)S(1)} fusion(f32[2,58,31,512]{3,2,1,0:T(8,128)} %get-tuple-element.15, f32[2,58,1,512]{3,2,1,0:T(1,128)S(1)} %get-tuple-element.17, f32[2,58,1,512]{3,2,1,0:T(1,128)S(1)} %get-tuple-element.16, f32[2,58,31,512]{3,2,1,0:T(8,128)S(1)} %get-tuple-element.14, f32[1,58,32,512]{3,2,1,0:T(8,128)S(1)} %get-tuple-element.8, ...), kind=kLoop, calls=%fused_computation.41 | loop fusion | flops 28508160 | bytes 45850624 | tf_op jit(solution)/shard_map/add | solution.py:50
  110.5 1.9 %slice_add_fusion = (f32[1,58,32,512]{3,2,1,0:T(8,128)S(1)}, f32[1,58,32,512]{3,2,1,0:T(8,128)S(1)}) fusion(f32[2,58,32,512]{3,2,1,0:T(8,128)S(1)} %fusion.14, f32[58,512]{1,0:T(8,128)S(1)} %fusion.40, f32[58]{0:T(128)S(1)} %multiply_subtract_fusion), kind=kLoop, calls=%fused_computation.49 | loop fusion | flops 5701632 | bytes 15323368 | tf_op jit(solution)/shard_map/add | solution.py:52
  112.5 1.5 fusion.18
  114.5 0.9 copy-done.2
  115.6 3.5 %gather_fusion = f32[1024,144]{1,0:T(8,128)S(1)} fusion(f32[144,512]{0,1:T(8,128)S(1)} %copy.31, s32[1024]{0:T(1024)S(1)} %broadcast_clamp_fusion.1), kind=kCustom, calls=%fused_computation | custom fusion | bytes 1183744 | tf_op jit(solution)/shard_map/gather | solution.py:118
  138.8 3.6 %all-to-all-start.2 = ((f32[32,144,32]{1,2,0:T(8,128)}), f32[32,144,32]{1,2,0:T(8,128)S(1)}, u32[]{:S(2)}, u32[]{:S(2)}) async-start(f32[32,144,32]{1,2,0:T(8,128)} %constant_dynamic-update-slice_fusion), calls=%async_computation.2 | async-start | bytes 2097152 | tf_op jit(solution)/shard_map/all_to_all | solution.py:120
  143.0 25.7 %all-to-all-done.2 = f32[32,144,32]{1,2,0:T(8,128)S(1)} async-done(((f32[32,144,32]{1,2,0:T(8,128)}), f32[32,144,32]{1,2,0:T(8,128)S(1)}, u32[]{:S(2)}, u32[]{:S(2)}) %all-to-all-start.2) | async-done | bytes 589856 | tf_op jit(solution)/shard_map/all_to_all | solution.py:120
  168.7 1.6 gather_fusion.1
  171.6 5.3 %collective-permute-start.1 = (f32[144,128]{0,1:T(8,128)S(1)}, f32[144,128]{0,1:T(8,128)S(1)}, u32[]{:S(2)}, u32[]{:S(2)}) collective-permute-start(f32[144,128]{0,1:T(8,128)S(1)} %broadcast_multiply_fusion), channel_id=1, source_target_pairs={{1,0},{2,1},{3,2},{4,3},{5,4},{6,5},{7,6},{8,7},{9,8},{10,9},{11,1... | collective-permute-start | bytes 221192 | tf_op jit(solution)/shard_map/ppermute | solution.py:26
  176.9 5.8 %fusion.19 = bf16[2,58,32,512]{3,2,1,0:T(8,128)(2,1)} fusion(f32[1,58,32,512]{3,2,1,0:T(8,128)} %copy-done.2, f32[1,58,32,512]{3,2,1,0:T(8,128)} %copy-done.1), kind=kLoop, calls=%fused_computation.48 | loop fusion | flops 1900544 | bytes 11403264 | tf_op jit(solution)/shard_map/convert_element_type | solution.py:64
  182.7 3.5 %gather_fusion.2 = f32[1024,144]{1,0:T(8,128)S(1)} fusion(f32[144,384]{0,1:T(8,128)S(1)} %pad_maximum_fusion.2, s32[1024]{0:T(1024)S(1)} %broadcast_clamp_fusion), kind=kCustom, calls=%fused_computation.2 | custom fusion | bytes 1183744 | tf_op jit(solution)/shard_map/jit(_take)/gather | solution.py:130
  186.2 0.7 fusion.25
  187.7 0.8 add.213
  (94 shorter events, 25.6 us)
Async XLA Ops:
  7.6 29.8 %all-to-all-start = ((f32[2,32,32]{2,0,1:T(2,128)}), f32[2,32,32]{2,0,1:T(2,128)S(1)}, u32[]{:S(2)}, u32[]{:S(2)}) async-start(f32[2,32,32]{2,0,1:T(2,128)} %copy.28), calls=%async_computation | async-start | bytes 65536 | tf_op jit(solution)/shard_map/all_to_all | solution.py:97
  14.9 11.3 %copy-start = (bf16[2,58,32,512]{3,2,1,0:T(8,128)(2,1)S(1)}, bf16[2,58,32,512]{3,2,1,0:T(8,128)(2,1)}, u32[]{:S(2)}) copy-start(bf16[2,58,32,512]{3,2,1,0:T(8,128)(2,1)} %param.6) | copy-start | bytes 11403268
  26.2 7.7 %copy-start.3 = (f32[2,72,512]{2,1,0:T(8,128)S(1)}, f32[2,72,512]{2,1,0:T(8,128)}, u32[]{:S(2)}) copy-start(f32[2,72,512]{2,1,0:T(8,128)} %param.5) | copy-start | bytes 884740
  37.4 32.1 %all-to-all-start.1 = ((f32[144,32,32]{0,2,1:T(8,128)}), f32[144,32,32]{0,2,1:T(8,128)S(1)}, u32[]{:S(2)}, u32[]{:S(2)}) async-start(f32[144,32,32]{0,2,1:T(8,128)} %bitcast.9), calls=%async_computation.1 | async-start | bytes 2097152 | tf_op jit(solution)/shard_map/all_to_all | solution.py:96
  112.4 2.0 %copy-start.1 = (f32[1,58,32,512]{3,2,1,0:T(8,128)}, f32[1,58,32,512]{3,2,1,0:T(8,128)S(1)}, u32[]{:S(2)}) copy-start(f32[1,58,32,512]{3,2,1,0:T(8,128)S(1)} %get-tuple-element.6) | copy-start | bytes 11403268
  112.5 2.9 %copy-start.2 = (f32[1,58,32,512]{3,2,1,0:T(8,128)}, f32[1,58,32,512]{3,2,1,0:T(8,128)S(1)}, u32[]{:S(2)}) copy-start(f32[1,58,32,512]{3,2,1,0:T(8,128)S(1)} %get-tuple-element.7) | copy-start | bytes 11403268
  112.5 30.0 %copy-start.4 = (s32[128,8]{0,1:T(8,128)S(1)}, s32[128,8]{0,1:T(8,128)}, u32[]{:S(2)}) copy-start(s32[128,8]{0,1:T(8,128)} %param.9) | copy-start | bytes 12292
  138.8 29.9 %all-to-all-start.2 = ((f32[32,144,32]{1,2,0:T(8,128)}), f32[32,144,32]{1,2,0:T(8,128)S(1)}, u32[]{:S(2)}, u32[]{:S(2)}) async-start(f32[32,144,32]{1,2,0:T(8,128)} %constant_dynamic-update-slice_fusion), calls=%async_computation.2 | async-start | bytes 2097152 | tf_op jit(solution)/shard_map/all_to_all | solution.py:120
  171.5 11.2 %collective-permute-start = (f32[144,128]{0,1:T(8,128)S(1)}, f32[144,128]{0,1:T(8,128)S(1)}, u32[]{:S(2)}, u32[]{:S(2)}) collective-permute-start(f32[144,128]{0,1:T(8,128)S(1)} %broadcast_multiply_fusion), channel_id=1, source_target_pairs={{0,1},{1,2},{2,3},{3,4},{4,5},{5,6},{6,7},{7,8},{8,9},{9,10},{10,1... | collective-permute-start | bytes 221192 | tf_op jit(solution)/shard_map/ppermute | solution.py:25
  171.6 11.1 %collective-permute-start.1 = (f32[144,128]{0,1:T(8,128)S(1)}, f32[144,128]{0,1:T(8,128)S(1)}, u32[]{:S(2)}, u32[]{:S(2)}) collective-permute-start(f32[144,128]{0,1:T(8,128)S(1)} %broadcast_multiply_fusion), channel_id=1, source_target_pairs={{1,0},{2,1},{3,2},{4,3},{5,4},{6,5},{7,6},{8,7},{9,8},{10,9},{11,1... | collective-permute-start | bytes 221192 | tf_op jit(solution)/shard_map/ppermute | solution.py:26
